TPU v7x, 256 devices: a whole 4x4x8 slice. The times are simulated.
256 devices in a mesh: pipe: 4 (over y_lo, core), ctx: 16 (over z, y_hi), tp: 4 (over x).
Axes of the slice: x: 4, y: 4 (y_hi: 2, y_lo: 2; y = y_hi * 2 + y_lo), z: 8, core: 2. Of those that a mesh axis runs over, the one named last changes fastest.
Arguments:
- segment_inputs: bfloat16 [4, 2, 2048, 4096], P('pipe', None, ('ctx', 'tp')), may hold values from -128 to 128
- keys: bfloat16 [4, 2, 2048, 512], P('pipe', None, 'ctx', 'tp'), may hold values from -64 to 64
- values: bfloat16 [4, 2, 2048, 512], P('pipe', None, 'ctx', 'tp'), may hold values from -6 to 6
- norm_gain: float32 [4, 4096], P('pipe'), may hold values from 0.1 to 1.9
- waiting_grads: bfloat16 [4, 2048, 4096], P('pipe', ('ctx', 'tp')), may hold values from -32 to 32
- output_grads: bfloat16 [1, 2048, 4096], P(None, ('ctx', 'tp')), may hold values from -32 to 32
- doc_lengths: int32 [5, 8], replicated, may hold values from 1 to 1024, as said below
Outputs:
- input_grads: bfloat16 [4, 2, 2048, 4096], P('pipe', None, ('ctx', 'tp'))
- key_grads: float32 [4, 2, 2048, 512], P('pipe', None, 'ctx', 'tp')
- value_grads: float32 [4, 2, 2048, 512], P('pipe', None, 'ctx', 'tp')
- gain_grads: float32 [4, 4096], P('pipe')
Inputs may be any that keep to these rules, and one draw needn't show every extreme that they name: `doc_lengths`: row m lists in order of position the lengths of the 8 documents packed into microbatch m's sequence; each row sums to 2048; the last document is exactly 1024 long.
All inputs are finite; a program needn't handle non-finite values.
Results may differ from a plain program's by a relative error of at most 0.009.
The roundings to bfloat16 on the way count: a program that leaves them out, or rounds other values in their place, can miss the bound.
Values may be sent and summed in bfloat16 or wider, within the bound.
A program may use at most 64 MiB of HBM per device.

v0:
```python
import jax
import jax.numpy as jnp
from jax import lax
from jax.sharding import PartitionSpec as P

HD = 128
S_DEV = 128
TICKS = 2
epsilon = 1e-05
masked_fill = -1e30


def passed_along(value, axis, by):
    count = lax.axis_size(axis)
    return lax.ppermute(value, axis, [(i, (i + by) % count) for i in range(count)])


def from_behind(value, axis, steps):
    count = lax.axis_size(axis)
    first, last = (max(0, -steps), min(count, count - steps))
    return lax.ppermute(value, axis, [(source, source + steps) for source in range(first, last)])


def row_positions(rows, half_rows, cycle_count):
    section = rows // half_rows
    offset = rows % half_rows
    owner = section // 2
    placed = jnp.where(section % 2 == 0, owner, 2 * cycle_count - 1 - owner)
    return placed * half_rows + offset


def document_starts(lengths_row, positions):
    closing = jnp.cumsum(lengths_row)
    passed = closing[None, :] <= positions[:, None]
    return jnp.sum(jnp.where(passed, lengths_row[None, :], 0), axis=1)


def keep_same(current):
    return current


def key_positions(key_first, key_count, cycle_count):
    rows = key_first + jnp.arange(key_count, dtype=jnp.int32)
    return row_positions(rows, S_DEV // 2, cycle_count)


def block_active(key_first, key_count, query_pos, query_start, cycle_count):
    key_pos = key_positions(key_first, key_count, cycle_count)
    return (jnp.min(key_pos) <= jnp.max(query_pos)) & (jnp.max(key_pos) >= jnp.min(query_start))


def score_block(query_block, key_block, query_pos, query_start, key_first, cycle_count):
    key_count = key_block.shape[0]
    key_pos = key_positions(key_first, key_count, cycle_count)
    scores = HD ** (-0.5) * jnp.einsum(
        "rkgd,skd->kgrs", query_block, key_block, preferred_element_type=jnp.float32
    )
    visible = (key_pos[None, :] <= query_pos[:, None]) & (key_pos[None, :] >= query_start[:, None])
    return (scores, visible[None, None])


def forward_update(carry, key_flat, value_flat, key_first, context):
    query_block, grad_block, query_pos, query_start, cycle_count = context
    key_count = key_flat.shape[0]

    def apply_block(current):
        row_peak, row_total, weighted = current
        key_block = key_flat.reshape(key_count, -1, HD)
        value_block = value_flat.reshape(key_count, -1, HD)
        scores, visible = score_block(
            query_block, key_block, query_pos, query_start, key_first, cycle_count
        )
        block_peak = jnp.max(jnp.where(visible, scores, masked_fill), axis=-1)
        new_peak = jnp.maximum(row_peak, block_peak)
        weights = jnp.where(visible, jnp.exp(scores - new_peak[..., None]), 0.0)
        prob_grad = jnp.einsum(
            "rkgd,skd->kgrs", grad_block, value_block, preferred_element_type=jnp.float32
        )
        return (new_peak, jnp.sum(weights, axis=-1), jnp.sum(weights * prob_grad, axis=-1))

    return lax.cond(
        block_active(key_first, key_count, query_pos, query_start, cycle_count),
        apply_block,
        keep_same,
        carry,
    )


def backward_terms(key_flat, value_flat, key_first, context, row_stats):
    query_block, grad_block, query_pos, query_start, cycle_count = context
    logsum, row_term = row_stats
    key_count = key_flat.shape[0]
    key_block = key_flat.reshape(key_count, -1, HD)
    value_block = value_flat.reshape(key_count, -1, HD)
    scale_factor = HD ** (-0.5)
    scores, visible = score_block(
        query_block, key_block, query_pos, query_start, key_first, cycle_count
    )
    prob_weights = jnp.where(visible, jnp.exp(scores - logsum[..., None]), 0.0)
    prob_grad = jnp.einsum(
        "rkgd,skd->kgrs", grad_block, value_block, preferred_element_type=jnp.float32
    )
    dscore = (prob_weights * (prob_grad - row_term[..., None])).astype(jnp.bfloat16)
    probs_low = prob_weights.astype(jnp.bfloat16)
    query_add = scale_factor * jnp.einsum(
        "kgrs,skd->rkgd", dscore, key_block, preferred_element_type=jnp.float32
    )
    key_add = scale_factor * jnp.einsum(
        "kgrs,rkgd->skd", dscore, query_block, preferred_element_type=jnp.float32
    )
    value_add = jnp.einsum(
        "kgrs,rkgd->skd", probs_low, grad_block, preferred_element_type=jnp.float32
    )
    return (query_add, key_add.reshape(key_count, -1), value_add.reshape(key_count, -1))


def segment_tick(inputs, key_local, value_local, gain_row, arriving, lengths_row):
    widened = inputs.astype(jnp.float32)
    inverse = lax.rsqrt(jnp.mean(widened * widened, axis=-1, keepdims=True) + epsilon)
    normed = widened * inverse
    queries = (normed * gain_row[None, :]).astype(jnp.bfloat16)
    query_heads, grad_heads = (
        lax.all_to_all(queries, "tp", split_axis=1, concat_axis=0, tiled=True),
        lax.all_to_all(arriving, "tp", split_axis=1, concat_axis=0, tiled=True),
    )
    row_count = key_local.shape[0]
    kv_local = key_local.shape[1] // HD
    group_size = query_heads.shape[1] // (HD * kv_local)
    query_block = query_heads.reshape(row_count, kv_local, group_size, HD)
    grad_block = grad_heads.reshape(row_count, kv_local, group_size, HD)
    cycle_count = lax.axis_size("ctx")
    cycle_place = lax.axis_index("ctx")
    query_pos = key_positions(cycle_place * row_count, row_count, cycle_count)
    query_start = document_starts(lengths_row, query_pos)
    context = (query_block, grad_block, query_pos, query_start, cycle_count)
    empty_peak = jnp.full((kv_local, group_size, row_count), masked_fill, jnp.float32)
    zero_rows = jnp.zeros((kv_local, group_size, row_count), jnp.float32)
    initial = (empty_peak, zero_rows, zero_rows)
    row_peak, row_total, weighted = forward_update(
        initial,
        lax.all_gather(key_local, "ctx", axis=0, tiled=True),
        lax.all_gather(value_local, "ctx", axis=0, tiled=True),
        jnp.int32(0),
        context,
    )
    row_stats = (row_peak + jnp.log(row_total), weighted / row_total)
    query_zero = jnp.zeros((row_count, kv_local, group_size, HD), jnp.float32)

    def cycle_turn(cycle_step, carry):
        key_block, value_block, key_grad, value_grad, query_grad = carry
        owner_index = (cycle_place - cycle_step) % cycle_count
        block_first = owner_index * row_count

        def apply_terms(current):
            added_terms = backward_terms(key_block, value_block, block_first, context, row_stats)
            return (
                current[0] + added_terms[1],
                current[1] + added_terms[2],
                current[2] + added_terms[0],
            )

        key_grad, value_grad, query_grad = lax.cond(
            block_active(block_first, row_count, query_pos, query_start, cycle_count),
            apply_terms,
            keep_same,
            (key_grad, value_grad, query_grad),
        )
        key_block, value_block = passed_along((key_block, value_block), "ctx", 1)
        key_grad, value_grad = passed_along((key_grad, value_grad), "ctx", 1)
        return (key_block, value_block, key_grad, value_grad, query_grad)

    zero_kv = jnp.zeros(key_local.shape, jnp.float32)
    finished = lax.fori_loop(
        0, cycle_count, cycle_turn, (key_local, value_local, zero_kv, zero_kv, query_zero)
    )
    key_grad, value_grad, query_grad = (finished[2], finished[3], finished[4])
    query_low = query_grad.reshape(row_count, -1).astype(jnp.bfloat16)
    grad_rows = lax.all_to_all(query_low, "tp", split_axis=0, concat_axis=1, tiled=True)
    rounded = grad_rows.astype(jnp.float32)
    scaled = rounded * gain_row[None, :]
    coupling = jnp.mean(scaled * normed, axis=-1, keepdims=True)
    input_grad = (arriving.astype(jnp.float32) + inverse * (scaled - normed * coupling)).astype(
        jnp.bfloat16
    )
    gain_part = jnp.sum(rounded * normed, axis=0)
    return (input_grad, key_grad, value_grad, gain_part)


def on_device(segment_inputs, keys, values, norm_gain, waiting_grads, output_grads, doc_lengths):
    segment_index = lax.axis_index("pipe")
    last_segment = lax.axis_size("pipe") - 1
    gain_row = norm_gain[0]
    arriving = waiting_grads[0]
    input_list = []
    key_list = []
    value_list = []
    gain_running = jnp.zeros(gain_row.shape, jnp.float32)
    for tick_index in range(TICKS):
        micro_index = segment_index + tick_index
        lengths_row = lax.dynamic_index_in_dim(doc_lengths, micro_index, 0, keepdims=False)
        input_grad, key_grad, value_grad, gain_part = segment_tick(
            segment_inputs[0, tick_index],
            keys[0, tick_index],
            values[0, tick_index],
            gain_row,
            arriving,
            lengths_row,
        )
        input_list.append(input_grad)
        key_list.append(key_grad)
        value_list.append(value_grad)
        gain_running = gain_running + gain_part
        if tick_index + 1 < TICKS:
            arrived = from_behind(input_grad, "pipe", -1)
            arriving = jnp.where(segment_index == last_segment, output_grads[tick_index], arrived)
    gain_grads = lax.psum(gain_running, ("ctx", "tp"))
    return (
        jnp.stack(input_list)[None],
        jnp.stack(key_list)[None],
        jnp.stack(value_list)[None],
        gain_grads[None],
    )


def solution(mesh):
    in_specs = (
        P("pipe", None, ("ctx", "tp"), None),
        P("pipe", None, "ctx", "tp"),
        P("pipe", None, "ctx", "tp"),
        P("pipe", None),
        P("pipe", ("ctx", "tp"), None),
        P(None, ("ctx", "tp"), None),
        P(),
    )
    out_specs = (
        P("pipe", None, ("ctx", "tp"), None),
        P("pipe", None, "ctx", "tp"),
        P("pipe", None, "ctx", "tp"),
        P("pipe", None),
    )
    return jax.shard_map(
        on_device, mesh=mesh, in_specs=in_specs, out_specs=out_specs, check_vma=False
    )
```

profile of v0, /device:TPU:8, one launch (start us, length us, event | category | flops | bytes accessed | tf_op | source)
XLA Modules:
  0.0 1165.9 jit_solution(12238675916187327474)
XLA Ops:
  21.4 46.2 %all-gather = bf16[1,1,2048,128]{3,2,1,0:T(8,128)(2,1)S(1)} all-gather(bf16[1,1,128,128]{3,2,1,0:T(8,128)(2,1)S(1)} %get-tuple-element.1508), channel_id=2, replica_groups=mesh['pipe'=4,'ctx'=16,'tp'=4] {'ctx'}, dimensions={2}, use_global_device_ids=true | all-gather | bytes 557056 | tf_op jit(solution)/shard_map/all_gather | solution.py:141
  72.2 40.6 %all-gather.1 = bf16[1,1,2048,128]{3,2,1,0:T(8,128)(2,1)} all-gather(bf16[1,1,128,128]{3,2,1,0:T(8,128)(2,1)S(1)} %get-tuple-element.1495), channel_id=3, replica_groups=mesh['pipe'=4,'ctx'=16,'tp'=4] {'ctx'}, dimensions={2}, use_global_device_ids=true | all-gather | bytes 557056 | tf_op jit(solution)/shard_map/all_gather | solution.py:142
  113.0 6.8 conditional.4
  120.0 273.9 %while.50 = (s32[]{:T(128)}, bf16[128,128]{1,0:T(8,128)(2,1)S(1)}, bf16[128,128]{1,0:T(8,128)(2,1)S(1)}, f32[128,128]{1,0:T(8,128)S(1)}, f32[128,128]{1,0:T(8,12...) while((s32[]{:T(128)}, bf16[128,128]{1,0:T(8,128)(2,1)S(1)}, ...), condition=%wide.region_17.18_spmd.clone, body=%wide.region_12.17_spmd.clone.sunk | while | flops 169071120 | bytes 6050608 | solution.py:173
  211.9 4.9 collective-permute-start.3
  219.8 4.8 collective-permute-done
  249.4 4.5 collective-permute-start.1
  282.3 4.7 collective-permute-start.1
  386.3 4.7 collective-permute-start.1
  394.9 5.4 all-to-all-start.2
  400.3 6.7 all-to-all-done.2
  411.5 41.4 %all-gather.2 = bf16[1,1,2048,128]{3,2,1,0:T(8,128)(2,1)S(1)} all-gather(bf16[1,1,128,128]{3,2,1,0:T(8,128)(2,1)S(1)} %get-tuple-element.1505), channel_id=4, replica_groups=mesh['pipe'=4,'ctx'=16,'tp'=4] {'ctx'}, dimensions={2}, use_global_device_ids=true | all-gather | bytes 557056 | tf_op jit(solution)/shard_map/all_gather | solution.py:141
  454.9 41.8 %all-gather.3 = bf16[1,1,2048,128]{3,2,1,0:T(8,128)(2,1)} all-gather(bf16[1,1,128,128]{3,2,1,0:T(8,128)(2,1)S(1)} %get-tuple-element.1492), channel_id=5, replica_groups=mesh['pipe'=4,'ctx'=16,'tp'=4] {'ctx'}, dimensions={2}, use_global_device_ids=true | all-gather | bytes 557056 | tf_op jit(solution)/shard_map/all_gather | solution.py:142
  512.4 5.1 all-to-all-done.4
  518.6 6.9 conditional.5
  525.6 273.6 %while.51 = (s32[]{:T(128)}, bf16[128,128]{1,0:T(8,128)(2,1)S(1)}, bf16[128,128]{1,0:T(8,128)(2,1)S(1)}, f32[128,128]{1,0:T(8,128)S(1)}, f32[128,128]{1,0:T(8,12...) while((s32[]{:T(128)}, bf16[128,128]{1,0:T(8,128)(2,1)S(1)}, ...), condition=%wide.region_33.34_spmd.clone, body=%wide.region_28.33_spmd.clone.sunk | while | flops 169071120 | bytes 6050608 | solution.py:173
  550.4 4.7 collective-permute-start.5
  616.8 4.9 collective-permute-start.7
  624.7 4.5 collective-permute-done.4
  655.0 4.7 collective-permute-start.5
  753.7 4.9 collective-permute-start.7
  791.7 4.7 collective-permute-start.5
  805.0 5.3 all-to-all-done.5
  810.8 353.9 %psum.7 = f32[1,4096]{1,0:T(1,128)} all-reduce(f32[1,4096]{1,0:T(1,128)S(1)} %bitcast.426), channel_id=1, replica_groups=mesh['pipe'=4,'ctx'=16,'tp'=4] {'ctx','tp'}, use_global_device_ids=true, to_apply=%region_37.38 | all-reduce | flops 4096 | bytes 32768 | tf_op jit(solution)/shard_map/psum | solution.py:216
  (996 shorter events, 522.0 us)
Async XLA Ops:
  6.3 61.3 %all-to-all-start = ((bf16[32,4,1024]{2,0,1:T(8,128)(2,1)}), bf16[32,4,1024]{2,0,1:T(8,128)(2,1)S(1)}, u32[]{:S(2)}, u32[]{:S(2)}) async-start(bf16[32,4,1024]{2,0,1:T(8,128)(2,1)} %multiply_convert_fusion.1), calls=%async_computation | async-start | bytes 524288 | tf_op jit(solution)/shard_map/all_to_all | solution.py:123
  67.7 45.2 %all-to-all-start.1 = ((bf16[32,4,1024]{2,0,1:T(8,128)(2,1)}), bf16[32,4,1024]{2,0,1:T(8,128)(2,1)S(1)}, u32[]{:S(2)}, u32[]{:S(2)}) async-start(bf16[32,4,1024]{2,0,1:T(8,128)(2,1)} %copy.84), calls=%async_computation.1 | async-start | bytes 524288 | tf_op jit(solution)/shard_map/all_to_all | solution.py:124
  143.1 9.3 collective-permute-start.3
  157.8 9.0 collective-permute-start.2
  192.7 8.8 collective-permute-start.2
  245.0 9.0 collective-permute-start.2
  245.1 8.9 collective-permute-start.3
  279.8 9.8 collective-permute-start.3
  295.0 10.4 collective-permute-start.2
  346.5 9.0 collective-permute-start.2
  380.8 10.3 collective-permute-start.2
  381.0 10.1 collective-permute-start.3
  394.9 12.0 %all-to-all-start.2 = ((bf16[4,32,1024]{2,1,0:T(8,128)(2,1)}), bf16[4,32,1024]{2,1,0:T(8,128)(2,1)S(1)}, u32[]{:S(2)}, u32[]{:S(2)}) async-start(bf16[4,32,1024]{2,1,0:T(8,128)(2,1)} %convert_element_type.172), calls=%async_computation.2 | async-start | bytes 524288 | tf_op jit(solution)/shard_map/all_to_all | solution.py:178
  409.6 91.3 %collective-permute-start.8 = (bf16[32,4096]{1,0:T(8,128)(2,1)}, bf16[32,4096]{1,0:T(8,128)(2,1)}, u32[]{:S(2)}, u32[]{:S(2)}) collective-permute-start(bf16[32,4096]{1,0:T(8,128)(2,1)} %fusion.122), channel_id=1, source_target_pairs={{64,0},{128,64},{192,128},{65,1},{129,65},{193,129},{66,2},{130,66... | collective-permute-start | bytes 786440 | tf_op jit(solution)/shard_map/ppermute | solution.py:21
  496.7 10.1 all-to-all-start.3
  506.8 10.8 all-to-all-start.4
  562.7 9.6 collective-permute-start.6
  649.9 9.8 collective-permute-start.6
  650.0 9.8 collective-permute-start.7
  685.4 8.9 collective-permute-start.7
  700.6 9.8 collective-permute-start.6
  786.7 9.7 collective-permute-start.6
  786.8 9.6 collective-permute-start.7
  800.3 10.1 all-to-all-start.5
  (122 other events, 3979.3 us)
where the time goes:
time: 1170 us
  blocking collectives  524 us (45%)
  starting transfers between devices  263 us (22%)
  waiting for transfers between devices  180 us (15%)
  loops' own time  85 us (7%)
  other arithmetic  51.5 us (4%)
  matrix products  46.7 us (4%)
    psum x1, blocking collectives, on_device(): gain_grads = lax.psum(gain_running, ('ctx', 'tp'))  354 us
    ppermute x128, starting transfers between devices, passed_along(): lax.ppermute(value, axis, [(i, (i + by) % count) for i in range(count)])  236 us
    ppermute x128, waiting for transfers between devices, passed_along(): lax.ppermute(value, axis, [(i, (i + by) % count) for i in range(count)])  159 us
    all_gather x2, blocking collectives, segment_tick(): lax.all_gather(key_local, 'ctx', axis=0, tiled=True)  87.6 us
    all_gather x2, blocking collectives, segment_tick(): lax.all_gather(value_local, 'ctx', axis=0, tiled=True)  82.4 us
    another operation x2, loops' own time, segment_tick(): lax.fori_loop(0, cycle_count, cycle_turn, (key_local, value_local, zero_k...  82.4 us
    reduce_max x33, other arithmetic, block_active(): jnp.max(key_pos) >= jnp.min(query_start)  23.7 us
  transfers between devices with their start and end apart: 135, of which 110 were waited for; matrix products, arithmetic and copies ran while one was open for 1% of the time, Pallas kernels for 0%

commit v1 on v0

--- a/solution.py
+++ b/solution.py
@@ -213,7 +213,7 @@
         if tick_index + 1 < TICKS:
             arrived = from_behind(input_grad, "pipe", -1)
             arriving = jnp.where(segment_index == last_segment, output_grads[tick_index], arrived)
-    gain_grads = lax.psum(gain_running, ("ctx", "tp"))
+    gain_grads = lax.psum(lax.psum(gain_running, "tp"), "ctx")
     return (
         jnp.stack(input_list)[None],
         jnp.stack(key_list)[None],

time: 1170 us -> 904 us (0.77)
  blocking collectives: 524 us -> 260 us
    psum x1 -> x2, blocking collectives: 354 us -> 89.7 us  [on_device(): gain_grads = lax.psum(lax.psum(gain_running, 'tp'), 'ctx')]
  transfers between devices with their start and end apart: 135 -> 135, of which waited for: 110 -> 110; matrix products, arithmetic and copies ran while one was open for 1% -> 2% of each run, Pallas kernels for 0% -> 0%
where the time goes in v1:
time: 904 us; the launch traced here: 902 us
  starting transfers between devices  263 us (29%)
  blocking collectives  260 us (29%)
  waiting for transfers between devices  180 us (20%)
  loops' own time  85 us (9%)
  other arithmetic  51.5 us (6%)
  matrix products  46.7 us (5%)
  local copies, waits for them, and re-layouts  10.6 us (1%)
    ppermute x128, starting transfers between devices, passed_along(): lax.ppermute(value, axis, [(i, (i + by) % count) for i in range(count)])  236 us
    ppermute x128, waiting for transfers between devices, passed_along(): lax.ppermute(value, axis, [(i, (i + by) % count) for i in range(count)])  159 us
    psum x2, blocking collectives, on_device(): gain_grads = lax.psum(lax.psum(gain_running, 'tp'), 'ctx')  89.7 us
    all_gather x2, blocking collectives, segment_tick(): lax.all_gather(key_local, 'ctx', axis=0, tiled=True)  87.6 us
    all_gather x2, blocking collectives, segment_tick(): lax.all_gather(value_local, 'ctx', axis=0, tiled=True)  82.4 us
    another operation x2, loops' own time, segment_tick(): lax.fori_loop(0, cycle_count, cycle_turn, (key_local, value_local, zero_k...  82.4 us
    reduce_max x33, other arithmetic, block_active(): jnp.max(key_pos) >= jnp.min(query_start)  23.7 us
  transfers between devices with their start and end apart: 135, of which 110 were waited for; matrix products, arithmetic and copies ran while one was open for 2% of the time, Pallas kernels for 0%

profile of v1, /device:TPU:8, one launch (start us, length us, event | category | flops | bytes accessed | tf_op | source)
XLA Modules:
  0.0 901.7 jit_solution(529617668611639105)
XLA Ops:
  21.4 46.2 %all-gather = bf16[1,1,2048,128]{3,2,1,0:T(8,128)(2,1)S(1)} all-gather(bf16[1,1,128,128]{3,2,1,0:T(8,128)(2,1)S(1)} %get-tuple-element.1508), channel_id=2, replica_groups=mesh['pipe'=4,'ctx'=16,'tp'=4] {'ctx'}, dimensions={2}, use_global_device_ids=true | all-gather | bytes 557056 | tf_op jit(solution)/shard_map/all_gather | solution.py:141
  72.2 40.6 %all-gather.1 = bf16[1,1,2048,128]{3,2,1,0:T(8,128)(2,1)} all-gather(bf16[1,1,128,128]{3,2,1,0:T(8,128)(2,1)S(1)} %get-tuple-element.1495), channel_id=3, replica_groups=mesh['pipe'=4,'ctx'=16,'tp'=4] {'ctx'}, dimensions={2}, use_global_device_ids=true | all-gather | bytes 557056 | tf_op jit(solution)/shard_map/all_gather | solution.py:142
  113.0 6.8 conditional.4
  120.0 273.9 %while.50 = (s32[]{:T(128)}, bf16[128,128]{1,0:T(8,128)(2,1)S(1)}, bf16[128,128]{1,0:T(8,128)(2,1)S(1)}, f32[128,128]{1,0:T(8,128)S(1)}, f32[128,128]{1,0:T(8,12...) while((s32[]{:T(128)}, bf16[128,128]{1,0:T(8,128)(2,1)S(1)}, ...), condition=%wide.region_17.18_spmd.clone, body=%wide.region_12.17_spmd.clone.sunk | while | flops 169071120 | bytes 6050608 | solution.py:173
  211.9 4.9 collective-permute-start.3
  219.8 4.8 collective-permute-done
  249.4 4.5 collective-permute-start.1
  282.3 4.7 collective-permute-start.1
  386.3 4.7 collective-permute-start.1
  394.9 5.4 all-to-all-start.2
  400.3 6.7 all-to-all-done.2
  411.5 41.4 %all-gather.2 = bf16[1,1,2048,128]{3,2,1,0:T(8,128)(2,1)S(1)} all-gather(bf16[1,1,128,128]{3,2,1,0:T(8,128)(2,1)S(1)} %get-tuple-element.1505), channel_id=4, replica_groups=mesh['pipe'=4,'ctx'=16,'tp'=4] {'ctx'}, dimensions={2}, use_global_device_ids=true | all-gather | bytes 557056 | tf_op jit(solution)/shard_map/all_gather | solution.py:141
  454.9 41.8 %all-gather.3 = bf16[1,1,2048,128]{3,2,1,0:T(8,128)(2,1)} all-gather(bf16[1,1,128,128]{3,2,1,0:T(8,128)(2,1)S(1)} %get-tuple-element.1492), channel_id=5, replica_groups=mesh['pipe'=4,'ctx'=16,'tp'=4] {'ctx'}, dimensions={2}, use_global_device_ids=true | all-gather | bytes 557056 | tf_op jit(solution)/shard_map/all_gather | solution.py:142
  512.4 5.1 all-to-all-done.4
  518.6 6.9 conditional.5
  525.6 273.6 %while.51 = (s32[]{:T(128)}, bf16[128,128]{1,0:T(8,128)(2,1)S(1)}, bf16[128,128]{1,0:T(8,128)(2,1)S(1)}, f32[128,128]{1,0:T(8,128)S(1)}, f32[128,128]{1,0:T(8,12...) while((s32[]{:T(128)}, bf16[128,128]{1,0:T(8,128)(2,1)S(1)}, ...), condition=%wide.region_33.34_spmd.clone, body=%wide.region_28.33_spmd.clone.sunk | while | flops 169071120 | bytes 6050608 | solution.py:173
  550.4 4.7 collective-permute-start.5
  616.8 4.9 collective-permute-start.7
  655.0 4.7 collective-permute-start.5
  753.7 4.9 collective-permute-start.7
  791.7 4.7 collective-permute-start.5
  805.0 5.3 all-to-all-done.5
  810.8 15.3 %psum.14 = f32[4096]{0:T(1024)S(1)} all-reduce(f32[4096]{0:T(1024)S(1)} %bitcast.428), channel_id=1, replica_groups=mesh['pipe'=4,'ctx'=16,'tp'=4] {'tp'}, use_global_device_ids=true, to_apply=%region_37.38 | all-reduce | flops 4096 | bytes 32768 | tf_op jit(solution)/shard_map/psum | solution.py:216
  826.1 74.4 %psum.15 = f32[1,4096]{1,0:T(1,128)} all-reduce(f32[1,4096]{1,0:T(1,128)S(1)} %bitcast.429), channel_id=1, replica_groups=mesh['pipe'=4,'ctx'=16,'tp'=4] {'ctx'}, use_global_device_ids=true, to_apply=%region_38.39 | all-reduce | flops 4096 | bytes 32768 | tf_op jit(solution)/shard_map/psum | solution.py:216
  (997 shorter events, 526.5 us)
Async XLA Ops:
  6.3 61.3 %all-to-all-start = ((bf16[32,4,1024]{2,0,1:T(8,128)(2,1)}), bf16[32,4,1024]{2,0,1:T(8,128)(2,1)S(1)}, u32[]{:S(2)}, u32[]{:S(2)}) async-start(bf16[32,4,1024]{2,0,1:T(8,128)(2,1)} %multiply_convert_fusion.1), calls=%async_computation | async-start | bytes 524288 | tf_op jit(solution)/shard_map/all_to_all | solution.py:123
  67.7 45.2 %all-to-all-start.1 = ((bf16[32,4,1024]{2,0,1:T(8,128)(2,1)}), bf16[32,4,1024]{2,0,1:T(8,128)(2,1)S(1)}, u32[]{:S(2)}, u32[]{:S(2)}) async-start(bf16[32,4,1024]{2,0,1:T(8,128)(2,1)} %copy.84), calls=%async_computation.1 | async-start | bytes 524288 | tf_op jit(solution)/shard_map/all_to_all | solution.py:124
  143.1 9.3 %collective-permute-start.3 = (f32[128,128]{1,0:T(8,128)S(1)}, f32[128,128]{1,0:T(8,128)S(1)}, u32[]{:S(2)}, u32[]{:S(2)}) collective-permute-start(f32[128,128]{1,0:T(8,128)S(1)} %get-tuple-element.1701), channel_id=1, source_target_pairs={{0,4},{4,8},{8,12},{12,16},{16,20},{20,24},{24,28},{28,32},{32,36}... | collective-permute-start | bytes 196616 | tf_op jit(solution)/shard_map/while/body/eval_jaxpr/ppermute | solution.py:15
  157.8 9.0 collective-permute-start.2
  192.7 8.8 collective-permute-start.2
  245.0 9.0 collective-permute-start.2
  245.1 8.9 collective-permute-start.3
  279.8 9.8 %collective-permute-start.3 = (f32[128,128]{1,0:T(8,128)S(1)}, f32[128,128]{1,0:T(8,128)S(1)}, u32[]{:S(2)}, u32[]{:S(2)}) collective-permute-start(f32[128,128]{1,0:T(8,128)S(1)} %get-tuple-element.1701), channel_id=1, source_target_pairs={{0,4},{4,8},{8,12},{12,16},{16,20},{20,24},{24,28},{28,32},{32,36}... | collective-permute-start | bytes 196616 | tf_op jit(solution)/shard_map/while/body/eval_jaxpr/ppermute | solution.py:15
  295.0 10.4 %collective-permute-start.2 = (f32[128,128]{1,0:T(8,128)S(1)}, f32[128,128]{1,0:T(8,128)S(1)}, u32[]{:S(2)}, u32[]{:S(2)}) collective-permute-start(f32[128,128]{1,0:T(8,128)S(1)} %get-tuple-element.1700), channel_id=1, source_target_pairs={{0,4},{4,8},{8,12},{12,16},{16,20},{20,24},{24,28},{28,32},{32,36}... | collective-permute-start | bytes 196616 | tf_op jit(solution)/shard_map/while/body/eval_jaxpr/ppermute | solution.py:15
  346.5 9.0 collective-permute-start.2
  380.8 10.3 %collective-permute-start.2 = (f32[128,128]{1,0:T(8,128)S(1)}, f32[128,128]{1,0:T(8,128)S(1)}, u32[]{:S(2)}, u32[]{:S(2)}) collective-permute-start(f32[128,128]{1,0:T(8,128)S(1)} %get-tuple-element.1700), channel_id=1, source_target_pairs={{0,4},{4,8},{8,12},{12,16},{16,20},{20,24},{24,28},{28,32},{32,36}... | collective-permute-start | bytes 196616 | tf_op jit(solution)/shard_map/while/body/eval_jaxpr/ppermute | solution.py:15
  381.0 10.1 %collective-permute-start.3 = (f32[128,128]{1,0:T(8,128)S(1)}, f32[128,128]{1,0:T(8,128)S(1)}, u32[]{:S(2)}, u32[]{:S(2)}) collective-permute-start(f32[128,128]{1,0:T(8,128)S(1)} %get-tuple-element.1701), channel_id=1, source_target_pairs={{0,4},{4,8},{8,12},{12,16},{16,20},{20,24},{24,28},{28,32},{32,36}... | collective-permute-start | bytes 196616 | tf_op jit(solution)/shard_map/while/body/eval_jaxpr/ppermute | solution.py:15
  394.9 12.0 %all-to-all-start.2 = ((bf16[4,32,1024]{2,1,0:T(8,128)(2,1)}), bf16[4,32,1024]{2,1,0:T(8,128)(2,1)S(1)}, u32[]{:S(2)}, u32[]{:S(2)}) async-start(bf16[4,32,1024]{2,1,0:T(8,128)(2,1)} %convert_element_type.172), calls=%async_computation.2 | async-start | bytes 524288 | tf_op jit(solution)/shard_map/all_to_all | solution.py:178
  409.6 91.3 %collective-permute-start.8 = (bf16[32,4096]{1,0:T(8,128)(2,1)}, bf16[32,4096]{1,0:T(8,128)(2,1)}, u32[]{:S(2)}, u32[]{:S(2)}) collective-permute-start(bf16[32,4096]{1,0:T(8,128)(2,1)} %fusion.122), channel_id=1, source_target_pairs={{64,0},{128,64},{192,128},{65,1},{129,65},{193,129},{66,2},{130,66... | collective-permute-start | bytes 786440 | tf_op jit(solution)/shard_map/ppermute | solution.py:21
  496.7 10.1 %all-to-all-start.3 = ((bf16[32,4,1024]{2,0,1:T(8,128)(2,1)}), bf16[32,4,1024]{2,0,1:T(8,128)(2,1)S(1)}, u32[]{:S(2)}, u32[]{:S(2)}) async-start(bf16[32,4,1024]{2,0,1:T(8,128)(2,1)} %get-tuple-element.1500), calls=%async_computation.3 | async-start | bytes 524288 | tf_op jit(solution)/shard_map/all_to_all | solution.py:123
  506.8 10.8 %all-to-all-start.4 = ((bf16[32,4,1024]{2,0,1:T(8,128)(2,1)}), bf16[32,4,1024]{2,0,1:T(8,128)(2,1)}, u32[]{:S(2)}, u32[]{:S(2)}) async-start(bf16[32,4,1024]{2,0,1:T(8,128)(2,1)} %bitcast.397), calls=%async_computation.4 | async-start | bytes 524288 | tf_op jit(solution)/shard_map/all_to_all | solution.py:124
  562.7 9.6 %collective-permute-start.6 = (f32[128,128]{1,0:T(8,128)S(1)}, f32[128,128]{1,0:T(8,128)S(1)}, u32[]{:S(2)}, u32[]{:S(2)}) collective-permute-start(f32[128,128]{1,0:T(8,128)S(1)} %get-tuple-element.1724), channel_id=1, source_target_pairs={{0,4},{4,8},{8,12},{12,16},{16,20},{20,24},{24,28},{28,32},{32,36}... | collective-permute-start | bytes 196616 | tf_op jit(solution)/shard_map/while/body/eval_jaxpr/ppermute | solution.py:15
  649.9 9.8 %collective-permute-start.6 = (f32[128,128]{1,0:T(8,128)S(1)}, f32[128,128]{1,0:T(8,128)S(1)}, u32[]{:S(2)}, u32[]{:S(2)}) collective-permute-start(f32[128,128]{1,0:T(8,128)S(1)} %get-tuple-element.1724), channel_id=1, source_target_pairs={{0,4},{4,8},{8,12},{12,16},{16,20},{20,24},{24,28},{28,32},{32,36}... | collective-permute-start | bytes 196616 | tf_op jit(solution)/shard_map/while/body/eval_jaxpr/ppermute | solution.py:15
  650.0 9.8 %collective-permute-start.7 = (f32[128,128]{1,0:T(8,128)S(1)}, f32[128,128]{1,0:T(8,128)S(1)}, u32[]{:S(2)}, u32[]{:S(2)}) collective-permute-start(f32[128,128]{1,0:T(8,128)S(1)} %get-tuple-element.1725), channel_id=1, source_target_pairs={{0,4},{4,8},{8,12},{12,16},{16,20},{20,24},{24,28},{28,32},{32,36}... | collective-permute-start | bytes 196616 | tf_op jit(solution)/shard_map/while/body/eval_jaxpr/ppermute | solution.py:15
  685.4 8.9 collective-permute-start.7
  700.6 9.8 %collective-permute-start.6 = (f32[128,128]{1,0:T(8,128)S(1)}, f32[128,128]{1,0:T(8,128)S(1)}, u32[]{:S(2)}, u32[]{:S(2)}) collective-permute-start(f32[128,128]{1,0:T(8,128)S(1)} %get-tuple-element.1724), channel_id=1, source_target_pairs={{0,4},{4,8},{8,12},{12,16},{16,20},{20,24},{24,28},{28,32},{32,36}... | collective-permute-start | bytes 196616 | tf_op jit(solution)/shard_map/while/body/eval_jaxpr/ppermute | solution.py:15
  786.7 9.7 %collective-permute-start.6 = (f32[128,128]{1,0:T(8,128)S(1)}, f32[128,128]{1,0:T(8,128)S(1)}, u32[]{:S(2)}, u32[]{:S(2)}) collective-permute-start(f32[128,128]{1,0:T(8,128)S(1)} %get-tuple-element.1724), channel_id=1, source_target_pairs={{0,4},{4,8},{8,12},{12,16},{16,20},{20,24},{24,28},{28,32},{32,36}... | collective-permute-start | bytes 196616 | tf_op jit(solution)/shard_map/while/body/eval_jaxpr/ppermute | solution.py:15
  786.8 9.6 %collective-permute-start.7 = (f32[128,128]{1,0:T(8,128)S(1)}, f32[128,128]{1,0:T(8,128)S(1)}, u32[]{:S(2)}, u32[]{:S(2)}) collective-permute-start(f32[128,128]{1,0:T(8,128)S(1)} %get-tuple-element.1725), channel_id=1, source_target_pairs={{0,4},{4,8},{8,12},{12,16},{16,20},{20,24},{24,28},{28,32},{32,36}... | collective-permute-start | bytes 196616 | tf_op jit(solution)/shard_map/while/body/eval_jaxpr/ppermute | solution.py:15
  800.3 10.1 %all-to-all-start.5 = ((bf16[4,32,1024]{2,1,0:T(8,128)(2,1)}), bf16[4,32,1024]{2,1,0:T(8,128)(2,1)S(1)}, u32[]{:S(2)}, u32[]{:S(2)}) async-start(bf16[4,32,1024]{2,1,0:T(8,128)(2,1)} %convert_element_type.193), calls=%async_computation.5 | async-start | bytes 524288 | tf_op jit(solution)/shard_map/all_to_all | solution.py:178
  (122 other events, 3715.1 us)
